TPU v7x, 32 devices: a whole 2x2x4 slice. The times are simulated.
32 devices in a mesh: wide: 8 (over z, x), narrow: 4 (over y, core).
Axes of the slice: x: 2, y: 2, z: 4, core: 2. Of those that a mesh axis runs over, the one named last changes fastest.
Arguments:
- state: float32 [2, 2097152], P(None, ('wide', 'narrow')), may hold values from -6 to 6
- gates: float32 [8, 2, 128, 128], replicated, may hold values from -1 to 1, as said below
- gate_qubits: int32 [8, 7], replicated, may hold values from 7 to 15, as said below
- swap_order: int32 [9], replicated, may hold values from 7 to 15, as said below
Outputs:
- checkpoint: float32 [2, 2097152], P(None, ('wide', 'narrow'))
Inputs may be any that keep to these rules, and one draw needn't show every extreme that they name: `gate_qubits`: each row names 7 different qubits. `swap_order`: each number of the range appears once. Each gates[g, 0] + i gates[g, 1] is a unitary matrix.
All inputs are finite; a program needn't handle non-finite values.
Results may differ from a plain program's by a relative error of at most 0.0003.
Values sent between devices are 32-bit elements; how exact they have to be, the bound alone decides.
A program may use at most 64 MiB of HBM per device.

v0:
```python
import functools
import math

import jax
import jax.numpy as jnp
from jax import lax
from jax.experimental import pallas as pl
from jax.experimental.pallas import tpu as pltpu
from jax.sharding import PartitionSpec as P

LANE_QUBITS = 7
LANES = 2**LANE_QUBITS
CHUNKS = 2

companding = 16.0
companding_norm = math.log(16.0 + math.sqrt(257.0))

MESH = pl.DeviceIdType.MESH


def inverse_sinh(values):
    magnitude = jnp.abs(values)
    squared = magnitude * magnitude
    return jnp.sign(values) * jnp.log1p(magnitude + squared / (1.0 + jnp.sqrt(squared + 1.0)))


def kernel(
    n_wide,
    n_narrow,
    upper,
    gate_bits,
    stages,
    qubits_ref,
    swap_ref,
    state_ref,
    gates_ref,
    final_ref,
    ext_ref,
    state_v,
    gates_v,
    final_v,
    perms,
    mats,
    wide_out,
    wide_in,
    narrow_out,
    narrow_in,
    ext_out,
    ext_narrow,
    ext_mid,
    ext_wide,
    local_sem,
    gate_sem,
    wide_send,
    wide_recv,
    narrow_send,
    narrow_recv,
    ext_nsend,
    ext_nrecv,
    ext_wsend,
    ext_wrecv,
):
    rows = 2**upper
    gate_dim = 2**gate_bits
    rest = rows // gate_dim
    wide_bits = n_wide.bit_length() - 1
    narrow_bits = n_narrow.bit_length() - 1
    wide_me = lax.axis_index("wide")
    narrow_me = lax.axis_index("narrow")
    half = LANES // 2

    state_copy = pltpu.make_async_copy(state_ref, state_v, local_sem.at[0])
    state_copy.start()
    gate_copies = []
    for number in range(gates_v.shape[0]):
        copy = pltpu.make_async_copy(
            gates_ref.at[number], gates_v.at[number], gate_sem.at[number]
        )
        copy.start()
        gate_copies.append(copy)

    barrier = pltpu.get_barrier_semaphore()
    for apart in range(1, n_wide):
        pl.semaphore_signal(
            barrier,
            inc=1,
            device_id=(lax.rem(wide_me + apart, n_wide), narrow_me),
            device_id_type=MESH,
        )
    for apart in range(1, n_narrow):
        pl.semaphore_signal(
            barrier,
            inc=1,
            device_id=(wide_me, lax.rem(narrow_me + apart, n_narrow)),
            device_id_type=MESH,
        )

    def gate_layout(number):
        masks = [jnp.int32(1) << (qubits_ref[number, k] - LANE_QUBITS) for k in range(gate_bits)]
        left = jnp.int32(rows - 1)
        for mask in masks:
            left = left - mask
        for _ in range(upper - gate_bits):
            low = left & (-left)
            masks.append(low)
            left = left - low
        return masks

    def swap_layout(order):
        return [jnp.int32(1) << (swap_ref[k] - LANE_QUBITS) for k in order]

    natural = [jnp.int32(1 << k) for k in range(upper)]
    wide_layout = swap_layout(range(upper))
    narrow_layout = swap_layout(list(range(narrow_bits, upper)) + list(range(narrow_bits)))

    column = lax.broadcasted_iota(jnp.int32, (1, rows), 1)
    row = lax.broadcasted_iota(jnp.int32, (rows, rows), 0)

    def make_perm(slot, source, target):
        index = jnp.zeros((1, rows), jnp.int32)
        for k in range(upper):
            index = index + jnp.where((column & (1 << k)) != 0, source[k], 0)
        goal = jnp.zeros((1, rows), jnp.int32)
        for k in range(upper):
            goal = goal + jnp.where((index & target[k]) != 0, 1 << k, 0)
        perms[slot] = (row == goal).astype(jnp.float32).astype(jnp.bfloat16)

    def make_matrix(number):
        gate_copies[number].wait()
        whole = jnp.concatenate([gates_v[number, 0], gates_v[number, 1]], axis=1)
        high = whole.astype(jnp.bfloat16)
        low = (whole - high.astype(jnp.float32)).astype(jnp.bfloat16)
        mats[number, :gate_dim] = high
        mats[number, gate_dim:] = low

    sign = jnp.where(lax.broadcasted_iota(jnp.int32, (1, LANES), 1) < half, -1.0, 1.0)

    def permuted(values, slot):
        high = values.astype(jnp.bfloat16)
        low = (values - high.astype(jnp.float32)).astype(jnp.bfloat16)
        both = jnp.concatenate([high, low], axis=1)
        moved = jnp.dot(perms[slot], both, preferred_element_type=jnp.float32)
        return moved[:, :LANES], moved[:, LANES:]

    def stacked(values):
        turned = pltpu.roll(values, half, 1) * sign
        pieces = []
        for part in (values, turned):
            pieces.append(
                jnp.concatenate(
                    [part[k * gate_dim : (k + 1) * gate_dim] for k in range(rest)], axis=1
                ).astype(jnp.bfloat16)
            )
        return jnp.concatenate(pieces, axis=0)

    def gate(values, slot, number):
        high, low = permuted(values, slot)
        first = jnp.dot(mats[number], stacked(high), preferred_element_type=jnp.float32)
        second = jnp.dot(
            mats[number, :gate_dim], stacked(low), preferred_element_type=jnp.float32
        )
        mixed = first[:gate_dim] + (first[gate_dim:] + second)
        return jnp.concatenate(
            [mixed[:, k * LANES : (k + 1) * LANES] for k in range(rest)], axis=0
        )

    def moved(values, slot):
        high, low = permuted(values, slot)
        return high + low

    def wide_copy(chunk, apart):
        other = lax.rem(wide_me + apart, n_wide)
        return pltpu.make_async_remote_copy(
            src_ref=wide_out.at[chunk, other],
            dst_ref=wide_in.at[chunk, wide_me],
            send_sem=wide_send.at[chunk, apart - 1],
            recv_sem=wide_recv.at[chunk, apart - 1],
            device_id=(other, narrow_me),
            device_id_type=MESH,
        )

    def narrow_copy(chunk, apart):
        other = lax.rem(narrow_me + apart, n_narrow)
        return pltpu.make_async_remote_copy(
            src_ref=narrow_out.at[chunk, other],
            dst_ref=narrow_in.at[chunk, narrow_me],
            send_sem=narrow_send.at[chunk, apart - 1],
            recv_sem=narrow_recv.at[chunk, apart - 1],
            device_id=(wide_me, other),
            device_id_type=MESH,
        )

    slot = 0
    plan = []
    for numbers, leave in zip(stages, (wide_layout, narrow_layout, natural)):
        plan.append((slot, numbers, leave))
        slot += len(numbers) + 1

    def prepare(stage, layout):
        start, numbers, leave = plan[stage]
        for k, number in enumerate(numbers):
            target = gate_layout(number)
            make_perm(start + k, layout, target)
            make_matrix(number)
            layout = target
        make_perm(start + len(numbers), layout, leave)

    def run(values, stage):
        start, numbers, _ = plan[stage]
        for k, number in enumerate(numbers):
            values = gate(values, start + k, number)
        return moved(values, start + len(numbers))

    prepare(0, natural)
    state_copy.wait()
    real = state_v[pl.ds(0, rows, stride=2), :]
    imag = state_v[pl.ds(1, rows, stride=2), :]
    first_half = lax.broadcasted_iota(jnp.int32, (1, LANES), 1) < half
    pieces = (
        jnp.where(first_half, real, pltpu.roll(imag, half, 1)),
        jnp.where(first_half, pltpu.roll(real, half, 1), imag),
    )
    for chunk in range(CHUNKS):
        values = run(pieces[chunk], 0)
        wide_out[chunk] = values.reshape(n_wide, rows // n_wide, LANES)
        if chunk == 0:
            pl.semaphore_wait(barrier, n_wide + n_narrow - 2)
        for apart in range(1, n_wide):
            wide_copy(chunk, apart).start()
        wide_in[chunk, wide_me] = wide_out[chunk, wide_me]

    prepare(1, wide_layout)
    prepare(2, narrow_layout)
    for chunk in range(CHUNKS):
        for apart in range(1, n_wide):
            wide_copy(chunk, apart).wait_recv()
        values = run(wide_in[chunk].reshape(rows, LANES), 1)
        narrow_out[chunk] = values.reshape(n_narrow, rows // n_narrow, LANES)
        for apart in range(1, n_narrow):
            narrow_copy(chunk, apart).start()
        narrow_in[chunk, narrow_me] = narrow_out[chunk, narrow_me]

    results = []
    for chunk in range(CHUNKS):
        for apart in range(1, n_narrow):
            narrow_copy(chunk, apart).wait_recv()
        results.append(run(narrow_in[chunk].reshape(rows, LANES), 2))

    high = jnp.maximum(results[0], results[1]).reshape(rows // 8, 8, LANES).max(axis=0)
    low = jnp.minimum(results[0], results[1]).reshape(rows // 8, 8, LANES).min(axis=0)
    ext_out[0] = high
    ext_out[1] = -low

    def ext_narrow_copy(apart):
        return pltpu.make_async_remote_copy(
            src_ref=ext_out,
            dst_ref=ext_narrow.at[apart - 1],
            send_sem=ext_nsend.at[apart - 1],
            recv_sem=ext_nrecv.at[apart - 1],
            device_id=(wide_me, lax.rem(narrow_me + apart, n_narrow)),
            device_id_type=MESH,
        )

    def ext_wide_copy(apart):
        return pltpu.make_async_remote_copy(
            src_ref=ext_mid,
            dst_ref=ext_wide.at[apart - 1],
            send_sem=ext_wsend.at[apart - 1],
            recv_sem=ext_wrecv.at[apart - 1],
            device_id=(lax.rem(wide_me + apart, n_wide), narrow_me),
            device_id_type=MESH,
        )

    for apart in range(1, n_narrow):
        ext_narrow_copy(apart).start()
    first_half_final, second_half_final = results
    final_v[pl.ds(0, rows, stride=2), :] = jnp.where(
        first_half, first_half_final, pltpu.roll(second_half_final, half, 1)
    )
    final_v[pl.ds(1, rows, stride=2), :] = jnp.where(
        first_half, pltpu.roll(first_half_final, half, 1), second_half_final
    )
    final_copy = pltpu.make_async_copy(final_v, final_ref, local_sem.at[1])
    final_copy.start()
    total = ext_out[...]
    for apart in range(1, n_narrow):
        ext_narrow_copy(apart).wait_recv()
        total = jnp.maximum(total, ext_narrow[apart - 1])
    ext_mid[...] = total
    for apart in range(1, n_wide):
        ext_wide_copy(apart).start()
    for apart in range(1, n_wide):
        ext_wide_copy(apart).wait_recv()
        total = jnp.maximum(total, ext_wide[apart - 1])
    ext_ref[0:1] = jnp.full((1, LANES), jnp.max(total[0]))
    ext_ref[1:2] = jnp.full((1, LANES), jnp.max(total[1]))

    for chunk in range(CHUNKS):
        for apart in range(1, n_wide):
            wide_copy(chunk, apart).wait_send()
        for apart in range(1, n_narrow):
            narrow_copy(chunk, apart).wait_send()
    for apart in range(1, n_narrow):
        ext_narrow_copy(apart).wait_send()
    for apart in range(1, n_wide):
        ext_wide_copy(apart).wait_send()
    final_copy.wait()


def local(state, gates, gate_qubits, swap_order):
    n_wide = lax.axis_size("wide")
    n_narrow = lax.axis_size("narrow")
    upper = state.shape[1].bit_length() - 1 - LANE_QUBITS
    rows = 2**upper
    gate_count, gate_bits = gate_qubits.shape
    gate_dim = 2**gate_bits
    stages = (range(3), range(3, 6), range(6, gate_count))
    dma = pltpu.SemaphoreType.DMA
    woven = state.reshape(2, rows, LANES).transpose(1, 0, 2).reshape(2 * rows, LANES)
    final, extremes = pl.pallas_call(
        functools.partial(kernel, n_wide, n_narrow, upper, gate_bits, stages),
        out_shape=(
            jax.ShapeDtypeStruct((2 * rows, LANES), jnp.float32),
            jax.ShapeDtypeStruct((2, LANES), jnp.float32),
        ),
        in_specs=[
            pl.BlockSpec(memory_space=pltpu.SMEM),
            pl.BlockSpec(memory_space=pltpu.SMEM),
            pl.BlockSpec(memory_space=pl.ANY),
            pl.BlockSpec(memory_space=pl.ANY),
        ],
        out_specs=(
            pl.BlockSpec(memory_space=pl.ANY),
            pl.BlockSpec(memory_space=pltpu.VMEM),
        ),
        scratch_shapes=[
            pltpu.VMEM((2 * rows, LANES), jnp.float32),
            pltpu.VMEM(gates.shape, jnp.float32),
            pltpu.VMEM((2 * rows, LANES), jnp.float32),
            pltpu.VMEM((gate_count + 3, rows, rows), jnp.bfloat16),
            pltpu.VMEM((gate_count, 2 * gate_dim, 2 * gate_dim), jnp.bfloat16),
            pltpu.VMEM((CHUNKS, n_wide, rows // n_wide, LANES), jnp.float32),
            pltpu.VMEM((CHUNKS, n_wide, rows // n_wide, LANES), jnp.float32),
            pltpu.VMEM((CHUNKS, n_narrow, rows // n_narrow, LANES), jnp.float32),
            pltpu.VMEM((CHUNKS, n_narrow, rows // n_narrow, LANES), jnp.float32),
            pltpu.VMEM((2, 8, LANES), jnp.float32),
            pltpu.VMEM((n_narrow - 1, 2, 8, LANES), jnp.float32),
            pltpu.VMEM((2, 8, LANES), jnp.float32),
            pltpu.VMEM((n_wide - 1, 2, 8, LANES), jnp.float32),
            dma((2,)),
            dma((gate_count,)),
            dma((CHUNKS, n_wide - 1)),
            dma((CHUNKS, n_wide - 1)),
            dma((CHUNKS, n_narrow - 1)),
            dma((CHUNKS, n_narrow - 1)),
            dma((n_narrow - 1,)),
            dma((n_narrow - 1,)),
            dma((n_wide - 1,)),
            dma((n_wide - 1,)),
        ],
        compiler_params=pltpu.CompilerParams(
            collective_id=0, has_side_effects=True, vmem_limit_bytes=48 * 2**20
        ),
        name="gate_layers",
    )(gate_qubits, swap_order, woven, gates)
    final = final.reshape(rows, 2, LANES).transpose(1, 0, 2).reshape(state.shape)
    highest = extremes[0, 0]
    lowest = -extremes[1, 0]
    middle = (highest + lowest) * 0.5
    halfwidth = (highest - lowest) * 0.5 + 1e-06
    return inverse_sinh(companding * (final - middle) / halfwidth) / companding_norm


def solution(mesh):
    in_specs = (P(None, ("wide", "narrow")), P(), P(), P())
    out_specs = P(None, ("wide", "narrow"))
    return jax.shard_map(local, mesh=mesh, in_specs=in_specs, out_specs=out_specs, check_vma=False)
```

profile of v0, /device:TPU:0, one launch (start us, length us, event | category | flops | bytes accessed | tf_op | source)
XLA Modules:
  0.0 48.2 jit_solution(18378750337722819032)
XLA Ops:
  0.0 0.0 copy-start.3
  0.0 0.7 %copy-done.3 = s32[9]{0:T(128)S(1)} copy-done((s32[9]{0:T(128)S(1)}, s32[9]{0:T(128)}, u32[]{:S(2)}) %copy-start.3) | copy-done | bytes 60
  0.7 0.0 copy-start
  0.7 1.2 %copy-done = f32[8,2,128,128]{3,2,1,0:T(8,128)S(1)} copy-done((f32[8,2,128,128]{3,2,1,0:T(8,128)S(1)}, f32[8,2,128,128]{3,2,1,0:T(8,128)}, u32[]{:S(2)}) %copy-start) | copy-done | bytes 1048600
  1.9 0.0 copy-start.1
  1.9 1.0 %copy-done.1 = f32[2,65536]{1,0:T(2,128)S(1)} copy-done((f32[2,65536]{1,0:T(2,128)S(1)}, f32[2,65536]{1,0:T(2,128)}, u32[]{:S(2)}) %copy-start.1) | copy-done | bytes 524312
  2.9 0.0 copy-start.2
  2.9 0.7 %copy-done.2 = s32[8,7]{1,0:T(8,128)S(1)} copy-done((s32[8,7]{1,0:T(8,128)S(1)}, s32[8,7]{1,0:T(8,128)}, u32[]{:S(2)}) %copy-start.2) | copy-done | bytes 248
  3.6 39.4 %gate_layers.1 = (f32[1024,128]{1,0:T(8,128)S(1)}, f32[2,128]{1,0:T(2,128)S(1)}) custom-call(s32[8,7]{1,0:T(8,128)S(1)} %copy-done.2, s32[9]{0:T(128)S(1)} %copy-done.3, f32[1024,128]{1,0:T(8,128)S(1)} %bitcast.22, f32[8,2,128,128]{3,2,1,0:T(8,128)S(1)} %copy-done), custom_call_target="tpu_custom_call" | custom-call | tf_op jit(solution)/shard_map/gate_layers/pallas_call | solution.py:320
  43.0 0.6 %fusion.3 = (f32[1,1]{1,0:T(1,128)}, f32[1,1]{1,0:T(1,128)}) fusion(f32[2,128]{1,0:T(2,128)S(1)} %get-tuple-element.8), kind=kLoop, calls=%fused_computation.5 | loop fusion | bytes 16 | tf_op jit(solution)/shard_map/slice | solution.py:368
  45.7 0.2 fusion.2
  45.9 2.4 %multiply_multiply_fusion = f32[2,65536]{1,0:T(2,128)} fusion(f32[2,65536]{1,0:T(2,128)S(1)} %bitcast.24, f32[2,65536]{1,0:T(2,128)S(1)} %bitcast.25, f32[2,65536]{1,0:T(2,128)S(1)} %bitcast.23), kind=kLoop, calls=%fused_computation | loop fusion | flops 786432 | bytes 2097152 | tf_op jit(solution)/shard_map/div | solution.py:371
Async XLA Ops:
  0.0 0.7 %copy-start.3 = (s32[9]{0:T(128)S(1)}, s32[9]{0:T(128)}, u32[]{:S(2)}) copy-start(s32[9]{0:T(128)} %swap_ref.1) | copy-start | bytes 112
  0.7 1.2 %copy-start = (f32[8,2,128,128]{3,2,1,0:T(8,128)S(1)}, f32[8,2,128,128]{3,2,1,0:T(8,128)}, u32[]{:S(2)}) copy-start(f32[8,2,128,128]{3,2,1,0:T(8,128)} %gates_ref.1) | copy-start | bytes 3145732
  1.9 1.0 %copy-start.1 = (f32[2,65536]{1,0:T(2,128)S(1)}, f32[2,65536]{1,0:T(2,128)}, u32[]{:S(2)}) copy-start(f32[2,65536]{1,0:T(2,128)} %param.4) | copy-start | bytes 1572868
  2.9 0.7 %copy-start.2 = (s32[8,7]{1,0:T(8,128)S(1)}, s32[8,7]{1,0:T(8,128)}, u32[]{:S(2)}) copy-start(s32[8,7]{1,0:T(8,128)} %qubits_ref.1) | copy-start | bytes 676
where the time goes:
time: 48.5 us; the launch traced here: 48.2 us
  Pallas kernels  39.4 us (81%)
  local copies, waits for them, and re-layouts  4.2 us (9%)
  other arithmetic  2.57 us (5%)
  between operations  2.05 us (4%)
    pallas_call x1, Pallas kernels, local(): pl.pallas_call(functools.partial(kernel, n_wide, n_narrow, upper, gate_bi...  39.4 us
    unnamed x8, local copies, waits for them, and re-layouts  3.61 us
    div x1, other arithmetic, local(): inverse_sinh(companding * (final - middle) / halfwidth) / companding_norm  2.36 us

commit v1 on v0

--- a/solution.py
+++ b/solution.py
@@ -18,27 +18,21 @@
 MESH = pl.DeviceIdType.MESH
 
 
-def inverse_sinh(values):
-    magnitude = jnp.abs(values)
-    squared = magnitude * magnitude
-    return jnp.sign(values) * jnp.log1p(magnitude + squared / (1.0 + jnp.sqrt(squared + 1.0)))
-
-
 def kernel(
     n_wide,
     n_narrow,
     upper,
     gate_bits,
     stages,
+    qubits_hbm,
+    swap_hbm,
+    state_ref,
+    gates_ref,
+    out_ref,
     qubits_ref,
     swap_ref,
-    state_ref,
-    gates_ref,
-    final_ref,
-    ext_ref,
     state_v,
     gates_v,
-    final_v,
     perms,
     mats,
     wide_out,
@@ -46,19 +40,15 @@
     narrow_out,
     narrow_in,
     ext_out,
-    ext_narrow,
-    ext_mid,
-    ext_wide,
+    ext_in,
     local_sem,
     gate_sem,
     wide_send,
     wide_recv,
     narrow_send,
     narrow_recv,
-    ext_nsend,
-    ext_nrecv,
-    ext_wsend,
-    ext_wrecv,
+    ext_send,
+    ext_recv,
 ):
     rows = 2**upper
     gate_dim = 2**gate_bits
@@ -69,6 +59,10 @@
     narrow_me = lax.axis_index("narrow")
     half = LANES // 2
 
+    qubits_copy = pltpu.make_async_copy(qubits_hbm, qubits_ref, local_sem.at[1])
+    qubits_copy.start()
+    swap_copy = pltpu.make_async_copy(swap_hbm, swap_ref, local_sem.at[2])
+    swap_copy.start()
     state_copy = pltpu.make_async_copy(state_ref, state_v, local_sem.at[0])
     state_copy.start()
     gate_copies = []
@@ -80,20 +74,26 @@
         gate_copies.append(copy)
 
     barrier = pltpu.get_barrier_semaphore()
-    for apart in range(1, n_wide):
-        pl.semaphore_signal(
-            barrier,
-            inc=1,
-            device_id=(lax.rem(wide_me + apart, n_wide), narrow_me),
-            device_id_type=MESH,
-        )
-    for apart in range(1, n_narrow):
-        pl.semaphore_signal(
-            barrier,
-            inc=1,
-            device_id=(wide_me, lax.rem(narrow_me + apart, n_narrow)),
-            device_id_type=MESH,
-        )
+    devices = n_wide * n_narrow
+    flat_me = wide_me * n_narrow + narrow_me
+
+    def device_at(apart):
+        other = lax.rem(flat_me + apart, devices)
+        return (lax.div(other, n_narrow), lax.rem(other, n_narrow))
+
+    def for_others(step):
+        if devices <= 64:
+            for apart in range(1, devices):
+                step(apart)
+        else:
+            lax.fori_loop(1, devices, lambda apart, _: step(apart), None)
+
+    def greet(apart):
+        pl.semaphore_signal(barrier, inc=1, device_id=device_at(apart), device_id_type=MESH)
+
+    for_others(greet)
+    qubits_copy.wait()
+    swap_copy.wait()
 
     def gate_layout(number):
         masks = [jnp.int32(1) << (qubits_ref[number, k] - LANE_QUBITS) for k in range(gate_bits)]
@@ -224,7 +224,7 @@
         values = run(pieces[chunk], 0)
         wide_out[chunk] = values.reshape(n_wide, rows // n_wide, LANES)
         if chunk == 0:
-            pl.semaphore_wait(barrier, n_wide + n_narrow - 2)
+            pl.semaphore_wait(barrier, devices - 1)
         for apart in range(1, n_wide):
             wide_copy(chunk, apart).start()
         wide_in[chunk, wide_me] = wide_out[chunk, wide_me]
@@ -246,65 +246,44 @@
             narrow_copy(chunk, apart).wait_recv()
         results.append(run(narrow_in[chunk].reshape(rows, LANES), 2))
 
-    high = jnp.maximum(results[0], results[1]).reshape(rows // 8, 8, LANES).max(axis=0)
-    low = jnp.minimum(results[0], results[1]).reshape(rows // 8, 8, LANES).min(axis=0)
-    ext_out[0] = high
-    ext_out[1] = -low
-
-    def ext_narrow_copy(apart):
+    high = jnp.maximum(results[0], results[1]).max(axis=0, keepdims=True)
+    low = -jnp.minimum(results[0], results[1]).min(axis=0, keepdims=True)
+    high = jnp.maximum(high, pltpu.roll(high, half, 1))
+    low = jnp.maximum(low, pltpu.roll(low, half, 1))
+    ext_out[...] = jnp.where(first_half, high, low)
+
+    def ext_copy(apart):
         return pltpu.make_async_remote_copy(
             src_ref=ext_out,
-            dst_ref=ext_narrow.at[apart - 1],
-            send_sem=ext_nsend.at[apart - 1],
-            recv_sem=ext_nrecv.at[apart - 1],
-            device_id=(wide_me, lax.rem(narrow_me + apart, n_narrow)),
+            dst_ref=ext_in.at[apart - 1],
+            send_sem=ext_send.at[apart - 1],
+            recv_sem=ext_recv.at[apart - 1],
+            device_id=device_at(apart),
             device_id_type=MESH,
         )
 
-    def ext_wide_copy(apart):
-        return pltpu.make_async_remote_copy(
-            src_ref=ext_mid,
-            dst_ref=ext_wide.at[apart - 1],
-            send_sem=ext_wsend.at[apart - 1],
-            recv_sem=ext_wrecv.at[apart - 1],
-            device_id=(lax.rem(wide_me + apart, n_wide), narrow_me),
-            device_id_type=MESH,
-        )
-
-    for apart in range(1, n_narrow):
-        ext_narrow_copy(apart).start()
-    first_half_final, second_half_final = results
-    final_v[pl.ds(0, rows, stride=2), :] = jnp.where(
-        first_half, first_half_final, pltpu.roll(second_half_final, half, 1)
-    )
-    final_v[pl.ds(1, rows, stride=2), :] = jnp.where(
-        first_half, pltpu.roll(first_half_final, half, 1), second_half_final
-    )
-    final_copy = pltpu.make_async_copy(final_v, final_ref, local_sem.at[1])
-    final_copy.start()
-    total = ext_out[...]
-    for apart in range(1, n_narrow):
-        ext_narrow_copy(apart).wait_recv()
-        total = jnp.maximum(total, ext_narrow[apart - 1])
-    ext_mid[...] = total
-    for apart in range(1, n_wide):
-        ext_wide_copy(apart).start()
-    for apart in range(1, n_wide):
-        ext_wide_copy(apart).wait_recv()
-        total = jnp.maximum(total, ext_wide[apart - 1])
-    ext_ref[0:1] = jnp.full((1, LANES), jnp.max(total[0]))
-    ext_ref[1:2] = jnp.full((1, LANES), jnp.max(total[1]))
-
+    for_others(lambda apart: ext_copy(apart).start())
+    state_v[:rows] = jnp.where(first_half, results[0], pltpu.roll(results[1], half, 1))
+    state_v[rows:] = jnp.where(first_half, pltpu.roll(results[0], half, 1), results[1])
     for chunk in range(CHUNKS):
         for apart in range(1, n_wide):
             wide_copy(chunk, apart).wait_send()
         for apart in range(1, n_narrow):
             narrow_copy(chunk, apart).wait_send()
-    for apart in range(1, n_narrow):
-        ext_narrow_copy(apart).wait_send()
-    for apart in range(1, n_wide):
-        ext_wide_copy(apart).wait_send()
-    final_copy.wait()
+    for_others(lambda apart: ext_copy(apart).wait_recv())
+    total = jnp.maximum(ext_out[...], ext_in[...].max(axis=0))
+    highest = jnp.max(jnp.where(first_half, total, -jnp.inf), axis=1, keepdims=True)
+    lowest = -jnp.max(jnp.where(first_half, -jnp.inf, total), axis=1, keepdims=True)
+    middle = (highest + lowest) * 0.5
+    halfwidth = (highest - lowest) * 0.5 + 1e-06
+    scale = companding / halfwidth
+    for plane in range(2):
+        values = (state_v[plane * rows : (plane + 1) * rows] - middle) * scale
+        magnitude = jnp.abs(values)
+        squared = magnitude * magnitude + 1.0
+        grown = jnp.log(magnitude + squared * lax.rsqrt(squared)) * (1.0 / companding_norm)
+        out_ref[pl.ds(plane, rows, stride=2), :] = jnp.where(values < 0, -grown, grown)
+    for_others(lambda apart: ext_copy(apart).wait_send())
 
 
 def local(state, gates, gate_qubits, swap_order):
@@ -317,58 +296,39 @@
     stages = (range(3), range(3, 6), range(6, gate_count))
     dma = pltpu.SemaphoreType.DMA
     woven = state.reshape(2, rows, LANES).transpose(1, 0, 2).reshape(2 * rows, LANES)
-    final, extremes = pl.pallas_call(
+    final = pl.pallas_call(
         functools.partial(kernel, n_wide, n_narrow, upper, gate_bits, stages),
-        out_shape=(
-            jax.ShapeDtypeStruct((2 * rows, LANES), jnp.float32),
-            jax.ShapeDtypeStruct((2, LANES), jnp.float32),
-        ),
-        in_specs=[
-            pl.BlockSpec(memory_space=pltpu.SMEM),
-            pl.BlockSpec(memory_space=pltpu.SMEM),
-            pl.BlockSpec(memory_space=pl.ANY),
-            pl.BlockSpec(memory_space=pl.ANY),
-        ],
-        out_specs=(
-            pl.BlockSpec(memory_space=pl.ANY),
-            pl.BlockSpec(memory_space=pltpu.VMEM),
-        ),
+        out_shape=jax.ShapeDtypeStruct((2 * rows, LANES), jnp.float32),
+        in_specs=[pl.BlockSpec(memory_space=pltpu.HBM)] * 4,
+        out_specs=pl.BlockSpec(memory_space=pltpu.VMEM),
         scratch_shapes=[
+            pltpu.SMEM(gate_qubits.shape, jnp.int32),
+            pltpu.SMEM(swap_order.shape, jnp.int32),
             pltpu.VMEM((2 * rows, LANES), jnp.float32),
             pltpu.VMEM(gates.shape, jnp.float32),
-            pltpu.VMEM((2 * rows, LANES), jnp.float32),
             pltpu.VMEM((gate_count + 3, rows, rows), jnp.bfloat16),
             pltpu.VMEM((gate_count, 2 * gate_dim, 2 * gate_dim), jnp.bfloat16),
             pltpu.VMEM((CHUNKS, n_wide, rows // n_wide, LANES), jnp.float32),
             pltpu.VMEM((CHUNKS, n_wide, rows // n_wide, LANES), jnp.float32),
             pltpu.VMEM((CHUNKS, n_narrow, rows // n_narrow, LANES), jnp.float32),
             pltpu.VMEM((CHUNKS, n_narrow, rows // n_narrow, LANES), jnp.float32),
-            pltpu.VMEM((2, 8, LANES), jnp.float32),
-            pltpu.VMEM((n_narrow - 1, 2, 8, LANES), jnp.float32),
-            pltpu.VMEM((2, 8, LANES), jnp.float32),
-            pltpu.VMEM((n_wide - 1, 2, 8, LANES), jnp.float32),
-            dma((2,)),
+            pltpu.VMEM((1, LANES), jnp.float32),
+            pltpu.VMEM((n_wide * n_narrow - 1, 1, LANES), jnp.float32),
+            dma((3,)),
             dma((gate_count,)),
             dma((CHUNKS, n_wide - 1)),
             dma((CHUNKS, n_wide - 1)),
             dma((CHUNKS, n_narrow - 1)),
             dma((CHUNKS, n_narrow - 1)),
-            dma((n_narrow - 1,)),
-            dma((n_narrow - 1,)),
-            dma((n_wide - 1,)),
-            dma((n_wide - 1,)),
+            dma((n_wide * n_narrow - 1,)),
+            dma((n_wide * n_narrow - 1,)),
         ],
         compiler_params=pltpu.CompilerParams(
-            collective_id=0, has_side_effects=True, vmem_limit_bytes=48 * 2**20
+            collective_id=0, has_side_effects=True, vmem_limit_bytes=67043328
         ),
         name="gate_layers",
     )(gate_qubits, swap_order, woven, gates)
-    final = final.reshape(rows, 2, LANES).transpose(1, 0, 2).reshape(state.shape)
-    highest = extremes[0, 0]
-    lowest = -extremes[1, 0]
-    middle = (highest + lowest) * 0.5
-    halfwidth = (highest - lowest) * 0.5 + 1e-06
-    return inverse_sinh(companding * (final - middle) / halfwidth) / companding_norm
+    return final.reshape(rows, 2, LANES).transpose(1, 0, 2).reshape(state.shape)
 
 
 def solution(mesh):

time: 48.5 us -> 39.3 us (0.81)
  other arithmetic: 2.57 us -> 0 us
  local copies, waits for them, and re-layouts: 4.2 us -> 1.87 us
  Pallas kernels: 39.4 us -> 37.3 us
  between operations: 2.05 us -> 0.01 us
    div x1 -> x0, other arithmetic: 2.36 us -> none  [local(): inverse_sinh(companding * (final - middle) / halfwidth) / companding_norm]
    pallas_call x1, Pallas kernels: 39.4 us -> 37.3 us  [local(): pl.pallas_call(functools.partial(kernel, n_wide, n_narrow, upper, gate_bi...]
    unnamed x8 -> x1, local copies, waits for them, and re-layouts: 3.61 us -> 1.87 us
    slice x1 -> x0, local copies, waits for them, and re-layouts: 0.59 us -> none  [local(): lowest = -extremes[1, 0]]
where the time goes in v1:
time: 39.3 us; the launch traced here: 39.2 us
  Pallas kernels  37.3 us (95%)
  local copies, waits for them, and re-layouts  1.87 us (5%)
    pallas_call x1, Pallas kernels, local(): pl.pallas_call(functools.partial(kernel, n_wide, n_narrow, upper, gate_bi...  37.3 us
    unnamed x1, local copies, waits for them, and re-layouts  1.87 us

profile of v1, /device:TPU:0, one launch (start us, length us, event | category | flops | bytes accessed | tf_op | source)
XLA Modules:
  0.0 39.2 jit_solution(7849579377863410456)
XLA Ops:
  0.0 37.3 %gate_layers.1 = f32[1024,128]{1,0:T(8,128)} custom-call(s32[8,7]{1,0:T(8,128)} %qubits_hbm.1, s32[9]{0:T(128)} %swap_hbm.1, f32[1024,128]{1,0:T(8,128)} %bitcast.11, f32[8,2,128,128]{3,2,1,0:T(8,128)} %gates_ref.1), custom_call_target="tpu_custom_call" | custom-call | tf_op jit(solution)/shard_map/gate_layers/pallas_call | solution.py:299
  37.3 1.9 %copy.8 = f32[2,65536]{1,0:T(2,128)} copy(f32[2,65536]{1,0:T(2,128)} %bitcast.10) | data formatting | bytes 1048576

commit v2 on v1

--- a/solution.py
+++ b/solution.py
@@ -10,7 +10,8 @@
 
 LANE_QUBITS = 7
 LANES = 2**LANE_QUBITS
-CHUNKS = 2
+WIDTHS = (LANES // 4, LANES // 2, LANES // 4)
+CHUNKS = len(WIDTHS)
 
 companding = 16.0
 companding_norm = math.log(16.0 + math.sqrt(257.0))
@@ -29,27 +30,31 @@
     state_ref,
     gates_ref,
     out_ref,
+    curve_ref,
     qubits_ref,
     swap_ref,
     state_v,
     gates_v,
+    final_v,
     perms,
     mats,
-    wide_out,
-    wide_in,
-    narrow_out,
-    narrow_in,
-    ext_out,
-    ext_in,
-    local_sem,
-    gate_sem,
-    wide_send,
-    wide_recv,
-    narrow_send,
-    narrow_recv,
-    ext_send,
-    ext_recv,
+    *rest_refs,
 ):
+    wide_out, wide_in, narrow_out, narrow_in = (
+        rest_refs[k * CHUNKS : (k + 1) * CHUNKS] for k in range(4)
+    )
+    (
+        ext_out,
+        ext_in,
+        local_sem,
+        gate_sem,
+        wide_send,
+        wide_recv,
+        narrow_send,
+        narrow_recv,
+        ext_send,
+        ext_recv,
+    ) = rest_refs[4 * CHUNKS :]
     rows = 2**upper
     gate_dim = 2**gate_bits
     rest = rows // gate_dim
@@ -133,17 +138,27 @@
         mats[number, :gate_dim] = high
         mats[number, gate_dim:] = low
 
-    sign = jnp.where(lax.broadcasted_iota(jnp.int32, (1, LANES), 1) < half, -1.0, 1.0)
-
-    def permuted(values, slot):
+    lane = lax.broadcasted_iota(jnp.int32, (1, LANES), 1)
+    first_half = lane < half
+
+    def permuted(values, slot, width):
         high = values.astype(jnp.bfloat16)
-        low = (values - high.astype(jnp.float32)).astype(jnp.bfloat16)
-        both = jnp.concatenate([high, low], axis=1)
-        moved = jnp.dot(perms[slot], both, preferred_element_type=jnp.float32)
-        return moved[:, :LANES], moved[:, LANES:]
-
-    def stacked(values):
-        turned = pltpu.roll(values, half, 1) * sign
+        low = values - high.astype(jnp.float32)
+        if width == half:
+            both = jnp.concatenate([high, low.astype(jnp.bfloat16)], axis=1)
+        else:
+            both = jnp.where(first_half, high.astype(jnp.float32), low).astype(jnp.bfloat16)
+        return jnp.dot(perms[slot], both, preferred_element_type=jnp.float32)
+
+    def stacked(values, width):
+        if width == half:
+            turned = pltpu.roll(values, half, 1) * jnp.where(first_half, -1.0, 1.0)
+        else:
+            turned = jnp.where(
+                lax.rem(lane, 2 * width) < width,
+                -pltpu.roll(values, LANES - width, 1),
+                pltpu.roll(values, width, 1),
+            )
         pieces = []
         for part in (values, turned):
             pieces.append(
@@ -153,26 +168,53 @@
             )
         return jnp.concatenate(pieces, axis=0)
 
-    def gate(values, slot, number):
-        high, low = permuted(values, slot)
-        first = jnp.dot(mats[number], stacked(high), preferred_element_type=jnp.float32)
-        second = jnp.dot(
-            mats[number, :gate_dim], stacked(low), preferred_element_type=jnp.float32
-        )
-        mixed = first[:gate_dim] + (first[gate_dim:] + second)
-        return jnp.concatenate(
+    def gate(values, slot, number, width):
+        both = permuted(values, slot, width)
+        if width == half:
+            first = jnp.dot(
+                mats[number], stacked(both[:, :LANES], width), preferred_element_type=jnp.float32
+            )
+            second = jnp.dot(
+                mats[number, :gate_dim],
+                stacked(both[:, LANES:], width),
+                preferred_element_type=jnp.float32,
+            )
+            mixed = first[:gate_dim] + (first[gate_dim:] + second)
+        else:
+            first = jnp.dot(mats[number], stacked(both, width), preferred_element_type=jnp.float32)
+            mixed = first[:gate_dim] + first[gate_dim:]
+        mixed = jnp.concatenate(
             [mixed[:, k * LANES : (k + 1) * LANES] for k in range(rest)], axis=0
         )
-
-    def moved(values, slot):
-        high, low = permuted(values, slot)
-        return high + low
+        return mixed if width == half else mixed + pltpu.roll(mixed, half, 1)
+
+    def moved(values, slot, width):
+        both = permuted(values, slot, width)
+        if width == half:
+            return both[:, :LANES] + both[:, LANES:]
+        return both + pltpu.roll(both, half, 1)
+
+    def packed(values, blocks, width):
+        values = values.reshape(blocks, rows // blocks, LANES)
+        if width == half:
+            return values
+        depth = rows // blocks // 2
+        return jnp.where(first_half, values[:, :depth], values[:, depth:])
+
+    def unpacked(values, width):
+        if width == half:
+            return values.reshape(rows, LANES)
+        blocks, depth, _ = values.shape
+        turned = pltpu.roll(values.reshape(blocks * depth, LANES), half, 1).reshape(values.shape)
+        return jnp.concatenate(
+            [jnp.where(first_half, values, turned), jnp.where(first_half, turned, values)], axis=1
+        ).reshape(rows, LANES)
 
     def wide_copy(chunk, apart):
         other = lax.rem(wide_me + apart, n_wide)
         return pltpu.make_async_remote_copy(
-            src_ref=wide_out.at[chunk, other],
-            dst_ref=wide_in.at[chunk, wide_me],
+            src_ref=wide_out[chunk].at[other],
+            dst_ref=wide_in[chunk].at[wide_me],
             send_sem=wide_send.at[chunk, apart - 1],
             recv_sem=wide_recv.at[chunk, apart - 1],
             device_id=(other, narrow_me),
@@ -182,8 +224,8 @@
     def narrow_copy(chunk, apart):
         other = lax.rem(narrow_me + apart, n_narrow)
         return pltpu.make_async_remote_copy(
-            src_ref=narrow_out.at[chunk, other],
-            dst_ref=narrow_in.at[chunk, narrow_me],
+            src_ref=narrow_out[chunk].at[other],
+            dst_ref=narrow_in[chunk].at[narrow_me],
             send_sem=narrow_send.at[chunk, apart - 1],
             recv_sem=narrow_recv.at[chunk, apart - 1],
             device_id=(wide_me, other),
@@ -205,49 +247,58 @@
             layout = target
         make_perm(start + len(numbers), layout, leave)
 
-    def run(values, stage):
+    def run(values, stage, width):
         start, numbers, _ = plan[stage]
         for k, number in enumerate(numbers):
-            values = gate(values, start + k, number)
-        return moved(values, start + len(numbers))
+            values = gate(values, start + k, number, width)
+        return moved(values, start + len(numbers), width)
+
+    def turn(values, by):
+        by = by % LANES
+        return values if by == 0 else pltpu.roll(values, by, 1)
+
+    firsts = [sum(WIDTHS[:chunk]) for chunk in range(CHUNKS)]
+
+    def piece(chunk):
+        width = WIDTHS[chunk]
+        values = None
+        for group in range(LANES // width):
+            part = turn((real, imag)[group % 2], group * width - firsts[chunk])
+            values = part if group == 0 else jnp.where(lane < group * width, values, part)
+        return values
 
     prepare(0, natural)
     state_copy.wait()
     real = state_v[pl.ds(0, rows, stride=2), :]
     imag = state_v[pl.ds(1, rows, stride=2), :]
-    first_half = lax.broadcasted_iota(jnp.int32, (1, LANES), 1) < half
-    pieces = (
-        jnp.where(first_half, real, pltpu.roll(imag, half, 1)),
-        jnp.where(first_half, pltpu.roll(real, half, 1), imag),
-    )
-    for chunk in range(CHUNKS):
-        values = run(pieces[chunk], 0)
-        wide_out[chunk] = values.reshape(n_wide, rows // n_wide, LANES)
+    for chunk, width in enumerate(WIDTHS):
+        values = run(piece(chunk), 0, width)
+        wide_out[chunk][...] = packed(values, n_wide, width)
         if chunk == 0:
             pl.semaphore_wait(barrier, devices - 1)
         for apart in range(1, n_wide):
             wide_copy(chunk, apart).start()
-        wide_in[chunk, wide_me] = wide_out[chunk, wide_me]
+        wide_in[chunk][wide_me] = wide_out[chunk][wide_me]
 
     prepare(1, wide_layout)
     prepare(2, narrow_layout)
-    for chunk in range(CHUNKS):
+    for chunk, width in enumerate(WIDTHS):
         for apart in range(1, n_wide):
             wide_copy(chunk, apart).wait_recv()
-        values = run(wide_in[chunk].reshape(rows, LANES), 1)
-        narrow_out[chunk] = values.reshape(n_narrow, rows // n_narrow, LANES)
+        values = run(unpacked(wide_in[chunk][...], width), 1, width)
+        narrow_out[chunk][...] = packed(values, n_narrow, width)
         for apart in range(1, n_narrow):
             narrow_copy(chunk, apart).start()
-        narrow_in[chunk, narrow_me] = narrow_out[chunk, narrow_me]
+        narrow_in[chunk][narrow_me] = narrow_out[chunk][narrow_me]
 
     results = []
-    for chunk in range(CHUNKS):
+    for chunk, width in enumerate(WIDTHS):
         for apart in range(1, n_narrow):
             narrow_copy(chunk, apart).wait_recv()
-        results.append(run(narrow_in[chunk].reshape(rows, LANES), 2))
-
-    high = jnp.maximum(results[0], results[1]).max(axis=0, keepdims=True)
-    low = -jnp.minimum(results[0], results[1]).min(axis=0, keepdims=True)
+        results.append(run(unpacked(narrow_in[chunk][...], width), 2, width))
+
+    high = functools.reduce(jnp.maximum, results).max(axis=0, keepdims=True)
+    low = -functools.reduce(jnp.minimum, results).min(axis=0, keepdims=True)
     high = jnp.maximum(high, pltpu.roll(high, half, 1))
     low = jnp.maximum(low, pltpu.roll(low, half, 1))
     ext_out[...] = jnp.where(first_half, high, low)
@@ -263,8 +314,14 @@
         )
 
     for_others(lambda apart: ext_copy(apart).start())
-    state_v[:rows] = jnp.where(first_half, results[0], pltpu.roll(results[1], half, 1))
-    state_v[rows:] = jnp.where(first_half, pltpu.roll(results[0], half, 1), results[1])
+    for plane in range(2):
+        values = None
+        for chunk, width in enumerate(WIDTHS):
+            part = turn(results[chunk], firsts[chunk] - plane * width)
+            values = part if chunk == 0 else jnp.where(lane < firsts[chunk], values, part)
+        final_v[pl.ds(plane, rows, stride=2), :] = values
+    final_copy = pltpu.make_async_copy(final_v, out_ref, local_sem.at[3])
+    final_copy.start()
     for chunk in range(CHUNKS):
         for apart in range(1, n_wide):
             wide_copy(chunk, apart).wait_send()
@@ -276,14 +333,20 @@
     lowest = -jnp.max(jnp.where(first_half, -jnp.inf, total), axis=1, keepdims=True)
     middle = (highest + lowest) * 0.5
     halfwidth = (highest - lowest) * 0.5 + 1e-06
-    scale = companding / halfwidth
-    for plane in range(2):
-        values = (state_v[plane * rows : (plane + 1) * rows] - middle) * scale
-        magnitude = jnp.abs(values)
-        squared = magnitude * magnitude + 1.0
-        grown = jnp.log(magnitude + squared * lax.rsqrt(squared)) * (1.0 / companding_norm)
-        out_ref[pl.ds(plane, rows, stride=2), :] = jnp.where(values < 0, -grown, grown)
+    curve_ref[...] = jnp.concatenate(
+        [jnp.broadcast_to(middle, (4, LANES)), jnp.broadcast_to(companding / halfwidth, (4, LANES))],
+        axis=0,
+    )
     for_others(lambda apart: ext_copy(apart).wait_send())
+    final_copy.wait()
+
+
+def compand(curve_ref, final_ref, out_ref):
+    values = (final_ref[...] - curve_ref[0:1]) * curve_ref[4:5]
+    magnitude = jnp.abs(values)
+    squared = magnitude * magnitude + 1.0
+    grown = jnp.log(magnitude + squared * lax.rsqrt(squared)) * (1.0 / companding_norm)
+    out_ref[...] = jnp.where(values < 0, -grown, grown)
 
 
 def local(state, gates, gate_qubits, swap_order):
@@ -296,25 +359,30 @@
     stages = (range(3), range(3, 6), range(6, gate_count))
     dma = pltpu.SemaphoreType.DMA
     woven = state.reshape(2, rows, LANES).transpose(1, 0, 2).reshape(2 * rows, LANES)
-    final = pl.pallas_call(
+    final, curve = pl.pallas_call(
         functools.partial(kernel, n_wide, n_narrow, upper, gate_bits, stages),
-        out_shape=jax.ShapeDtypeStruct((2 * rows, LANES), jnp.float32),
+        out_shape=(
+            jax.ShapeDtypeStruct((2 * rows, LANES), jnp.float32),
+            jax.ShapeDtypeStruct((8, LANES), jnp.float32),
+        ),
         in_specs=[pl.BlockSpec(memory_space=pltpu.HBM)] * 4,
-        out_specs=pl.BlockSpec(memory_space=pltpu.VMEM),
+        out_specs=(pl.BlockSpec(memory_space=pl.ANY), pl.BlockSpec(memory_space=pltpu.VMEM)),
         scratch_shapes=[
             pltpu.SMEM(gate_qubits.shape, jnp.int32),
             pltpu.SMEM(swap_order.shape, jnp.int32),
             pltpu.VMEM((2 * rows, LANES), jnp.float32),
             pltpu.VMEM(gates.shape, jnp.float32),
+            pltpu.VMEM((2 * rows, LANES), jnp.float32),
             pltpu.VMEM((gate_count + 3, rows, rows), jnp.bfloat16),
             pltpu.VMEM((gate_count, 2 * gate_dim, 2 * gate_dim), jnp.bfloat16),
-            pltpu.VMEM((CHUNKS, n_wide, rows // n_wide, LANES), jnp.float32),
-            pltpu.VMEM((CHUNKS, n_wide, rows // n_wide, LANES), jnp.float32),
-            pltpu.VMEM((CHUNKS, n_narrow, rows // n_narrow, LANES), jnp.float32),
-            pltpu.VMEM((CHUNKS, n_narrow, rows // n_narrow, LANES), jnp.float32),
+            *[
+                pltpu.VMEM((blocks, rows // blocks * 2 * width // LANES, LANES), jnp.float32)
+                for blocks in (n_wide, n_wide, n_narrow, n_narrow)
+                for width in WIDTHS
+            ],
             pltpu.VMEM((1, LANES), jnp.float32),
             pltpu.VMEM((n_wide * n_narrow - 1, 1, LANES), jnp.float32),
-            dma((3,)),
+            dma((4,)),
             dma((gate_count,)),
             dma((CHUNKS, n_wide - 1)),
             dma((CHUNKS, n_wide - 1)),
@@ -328,6 +396,16 @@
         ),
         name="gate_layers",
     )(gate_qubits, swap_order, woven, gates)
+    steps = 4
+    block = pl.BlockSpec((2 * rows // steps, LANES), lambda step: (step, 0))
+    final = pl.pallas_call(
+        compand,
+        grid=(steps,),
+        out_shape=jax.ShapeDtypeStruct((2 * rows, LANES), jnp.float32),
+        in_specs=[pl.BlockSpec((8, LANES), lambda step: (0, 0)), block],
+        out_specs=block,
+        name="compand",
+    )(curve, final)
     return final.reshape(rows, 2, LANES).transpose(1, 0, 2).reshape(state.shape)
 
 

time: 39.3 us -> 42.7 us (1.087)
  Pallas kernels: 37.3 us -> 42.5 us
  local copies, waits for them, and re-layouts: 1.87 us -> 0 us
    pallas_call x0 -> x1, Pallas kernels: none -> 3.29 us  [local(): pl.pallas_call(compand, grid=(steps,), out_shape=jax.ShapeDtypeStruct((2...]
    pallas_call x1, Pallas kernels: 37.3 us -> 39.2 us  [local(): pl.pallas_call(functools.partial(kernel, n_wide, n_narrow, upper, gate_bi...]
    unnamed x1 -> x0, local copies, waits for them, and re-layouts: 1.87 us -> none
where the time goes in v2:
time: 42.7 us; the launch traced here: 42.5 us
  Pallas kernels  42.5 us (100%)
    pallas_call x1, Pallas kernels, local(): pl.pallas_call(functools.partial(kernel, n_wide, n_narrow, upper, gate_bi...  39.2 us
    pallas_call x1, Pallas kernels, local(): pl.pallas_call(compand, grid=(steps,), out_shape=jax.ShapeDtypeStruct((2...  3.29 us

profile of v2, /device:TPU:0, one launch (start us, length us, event | category | flops | bytes accessed | tf_op | source)
XLA Modules:
  0.0 42.5 jit_solution(2709937302711373209)
XLA Ops:
  0.0 39.2 %gate_layers.1 = (f32[1024,128]{1,0:T(8,128)}, f32[8,128]{1,0:T(8,128)}) custom-call(s32[8,7]{1,0:T(8,128)} %qubits_hbm.1, s32[9]{0:T(128)} %swap_hbm.1, f32[1024,128]{1,0:T(8,128)} %bitcast.10, f32[8,2,128,128]{3,2,1,0:T(8,128)} %gates_ref.1), custom_call_target="tpu_custom_call" | custom-call | tf_op jit(solution)/shard_map/gate_layers/pallas_call | solution.py:362
  39.2 3.3 %compand.1 = f32[1024,128]{1,0:T(8,128)} custom-call(f32[8,128]{1,0:T(8,128)} %get-tuple-element.7.curve_ref, f32[1024,128]{1,0:T(8,128)} %get-tuple-element.8.final_ref), custom_call_target="tpu_custom_call" | custom-call | tf_op jit(solution)/shard_map/compand/pallas_call | solution.py:401

commit v3 on v1

--- a/solution.py
+++ b/solution.py
@@ -142,27 +142,25 @@
         moved = jnp.dot(perms[slot], both, preferred_element_type=jnp.float32)
         return moved[:, :LANES], moved[:, LANES:]
 
-    def stacked(values):
-        turned = pltpu.roll(values, half, 1) * sign
-        pieces = []
-        for part in (values, turned):
-            pieces.append(
-                jnp.concatenate(
-                    [part[k * gate_dim : (k + 1) * gate_dim] for k in range(rest)], axis=1
-                ).astype(jnp.bfloat16)
+    def gate(values, slot, number):
+        both = jnp.concatenate(permuted(values, slot), axis=1)
+        blocks = []
+        for k in range(rest):
+            part = both[k * gate_dim : (k + 1) * gate_dim]
+            turned = jnp.concatenate(
+                [
+                    pltpu.roll(part[:, :LANES], half, 1) * sign,
+                    pltpu.roll(part[:, LANES:], half, 1) * sign,
+                ],
+                axis=1,
             )
-        return jnp.concatenate(pieces, axis=0)
-
-    def gate(values, slot, number):
-        high, low = permuted(values, slot)
-        first = jnp.dot(mats[number], stacked(high), preferred_element_type=jnp.float32)
-        second = jnp.dot(
-            mats[number, :gate_dim], stacked(low), preferred_element_type=jnp.float32
-        )
-        mixed = first[:gate_dim] + (first[gate_dim:] + second)
-        return jnp.concatenate(
-            [mixed[:, k * LANES : (k + 1) * LANES] for k in range(rest)], axis=0
-        )
+            whole = jnp.concatenate([part, turned], axis=0).astype(jnp.bfloat16)
+            mixed = jnp.dot(mats[number], whole, preferred_element_type=jnp.float32)
+            blocks.append(
+                mixed[:gate_dim, :LANES]
+                + (mixed[gate_dim:, :LANES] + mixed[:gate_dim, LANES:])
+            )
+        return jnp.concatenate(blocks, axis=0)
 
     def moved(values, slot):
         high, low = permuted(values, slot)

time: 39.3 us -> 38.7 us (0.985)
  Pallas kernels: 37.3 us -> 36.7 us
    pallas_call x1, Pallas kernels: 37.3 us -> 36.7 us  [local(): pl.pallas_call(functools.partial(kernel, n_wide, n_narrow, upper, gate_bi...]
where the time goes in v3:
time: 38.7 us; the launch traced here: 38.5 us
  Pallas kernels  36.7 us (95%)
  local copies, waits for them, and re-layouts  1.87 us (5%)
    pallas_call x1, Pallas kernels, local(): pl.pallas_call(functools.partial(kernel, n_wide, n_narrow, upper, gate_bi...  36.7 us
    unnamed x1, local copies, waits for them, and re-layouts  1.87 us

profile of v3, /device:TPU:0, one launch (start us, length us, event | category | flops | bytes accessed | tf_op | source)
XLA Modules:
  0.0 38.5 jit_solution(3286320680342627993)
XLA Ops:
  0.0 36.7 %gate_layers.1 = f32[1024,128]{1,0:T(8,128)} custom-call(s32[8,7]{1,0:T(8,128)} %qubits_hbm.1, s32[9]{0:T(128)} %swap_hbm.1, f32[1024,128]{1,0:T(8,128)} %bitcast.11, f32[8,2,128,128]{3,2,1,0:T(8,128)} %gates_ref.1), custom_call_target="tpu_custom_call" | custom-call | tf_op jit(solution)/shard_map/gate_layers/pallas_call | solution.py:297
  36.7 1.9 %copy.8 = f32[2,65536]{1,0:T(2,128)} copy(f32[2,65536]{1,0:T(2,128)} %bitcast.10) | data formatting | bytes 1048576
